TPU v7x, 128 devices: a whole 4x4x4 slice. The times are simulated.
128 devices in a mesh: row: 32 (over x, y, core), col: 4 (over z).
Axes of the slice: x: 4, y: 4, z: 4, core: 2. Of those that a mesh axis runs over, the one named last changes fastest.
Arguments:
- right_side: bfloat16 [65536, 4096], P(('row', 'col')), may hold values from -6 to 6
- factor: bfloat16 [65536, 2048], P(('row', 'col')), may hold values from -0.125 to 0.125
- diag_inverse: bfloat16 [2048, 512], P('col'), as said below
- tile_mask: int32 [128, 4], P(('row', 'col')), may hold values from 0 to 1, as said below
- window_rows: int32 [4], replicated, may hold values from 0 to 127, as said below
Outputs:
- solution: bfloat16 [2048, 4096], P('row', 'col')
- updated_rhs: bfloat16 [65536, 4096], P(('row', 'col'))
Inputs may be any that keep to these rules, and one draw needn't show every extreme that they name: `window_rows`: distinct stored panel numbers, panels 0 and 127 always among them; panel p is stored on device p // 1 of row+col, and the window panels lie on different devices. `tile_mask`: 0 or 1; in the row of window panel k the entries of columns k and beyond are 0. `diag_inverse`: each tile is lower triangular.
All inputs are finite; a program needn't handle non-finite values.
Results may differ from a plain program's by a relative error of at most 0.0056.
Values may be sent and summed in bfloat16 or wider, within the bound.
A program may use at most 128 MiB of HBM per device.

v0:
```python
import jax
import jax.numpy as jnp
from jax import lax
from jax.sharding import PartitionSpec as P


def spread(block, axis, source):
    block = jnp.where(lax.axis_index(axis) == source, block, jnp.zeros_like(block))
    return lax.psum(block, axis)


def tile_term(flag, tile, panel_solution):
    zeros = jnp.zeros((tile.shape[0], panel_solution.shape[1]), jnp.float32)
    return lax.cond(
        flag > 0,
        lambda: jnp.dot(tile, panel_solution, preferred_element_type=jnp.float32),
        lambda: zeros,
    )


def body(right_side, factor, diag_inverse, tile_mask, window_rows):
    panel = diag_inverse.shape[1]
    window = factor.shape[1] // panel
    pan_dev = factor.shape[0] // panel
    columns = right_side.shape[1]
    ncol = lax.axis_size("col")
    nrow = lax.axis_size("row")
    inverses = lax.all_gather(diag_inverse, "col", axis=0, tiled=True).reshape(window, panel, panel)
    col_index = lax.axis_index("col")
    row_index = lax.axis_index("row")
    accum = jnp.zeros((pan_dev * panel, columns), jnp.float32)
    solved = []
    for k in range(window):
        target = window_rows[k]
        owner = target // pan_dev
        update = accum
        residual = right_side.astype(jnp.float32) - update
        rounded = residual.astype(jnp.bfloat16)
        local_solution = jnp.dot(inverses[k], rounded, preferred_element_type=jnp.float32).astype(
            jnp.bfloat16
        )
        solution_panel = spread(local_solution, ("row", "col"), owner)
        solved.append(solution_panel)
        tile = factor[0:panel, k * panel : (k + 1) * panel]
        term = tile_term(tile_mask[0, k], tile, solution_panel)
        accum = accum.at[0:panel].add(term)
    whole = jnp.concatenate(solved, axis=0)
    updated = (right_side.astype(jnp.float32) - accum).astype(jnp.bfloat16)
    block_rows = whole.shape[0] // nrow
    block_cols = columns // ncol
    solution = lax.dynamic_slice(
        whole, (row_index * block_rows, col_index * block_cols), (block_rows, block_cols)
    )
    return (solution, updated)


def solution(mesh):
    in_specs = (
        P(("row", "col"), None),
        P(("row", "col"), None),
        P("col", None),
        P(("row", "col"), None),
        P(),
    )
    out_specs = (P("row", "col"), P(("row", "col"), None))
    return jax.shard_map(body, mesh=mesh, in_specs=in_specs, out_specs=out_specs, check_vma=False)
```

profile of v0, /device:TPU:1, one launch (start us, length us, event | category | flops | bytes accessed | tf_op | source)
XLA Modules:
  0.0 760.8 jit_solution(18041693883802960980)
XLA Ops:
  7.2 0.0 all-gather.2.cloned.1.call-start
  7.2 0.7 all-gather.2.cloned.1.call-update
  7.9 0.0 all-reduce.5.cloned.1.call-start
  8.0 1.5 fusion.30
  10.1 33.9 %all-gather.2.cloned.1.call-done = bf16[2048,512]{1,0:T(8,128)(2,1)} async-done(((bf16[512,512]{1,0:T(8,128)(2,1)}), bf16[2048,512]{1,0:T(8,128)(2,1)}) %all-gather.2.cloned.1.call-update) | async-done | bytes 2097168 | tf_op jit(solution)/shard_map/all_gather | solution.py:28
  44.0 6.7 fusion.12
  50.7 0.0 copy-start.3
  50.7 0.0 copy-start.2
  50.7 0.0 all-reduce.5.cloned.1.call-update
  50.7 0.0 all-reduce.7.cloned.1.call-start
  50.8 0.6 copy-done.3
  51.3 0.7 fusion.29
  53.3 151.5 %all-reduce.5.cloned.1.call-done = bf16[512,4096]{1,0:T(8,128)(2,1)} async-done(((bf16[512,4096]{1,0:T(8,128)(2,1)}), bf16[512,4096]{1,0:T(8,128)(2,1)}) %all-reduce.5.cloned.1.call-update) | async-done | bytes 4194320 | tf_op jit(solution)/shard_map/psum | solution.py:9
  204.8 0.0 copy-done.2
  204.8 7.8 %conditional.4 = (f32[512,4096]{1,0:T(8,128)}) conditional(s32[]{:T(128)} %bitcast.2, () %tuple.68, (bf16[512,2048]{1,0:T(8,128)(2,1)S(1)}, bf16[512,4096]{1,0:T(8,128)(2,1)}) %tuple.101), branch_computations={%region_1.2_spmd, %region_2.3_spmd} | conditional | flops 2147483648 | bytes 13107208 | solution.py:14
  204.8 7.8 %fusion = f32[512,4096]{1,0:T(8,128)} fusion(bf16[512,4096]{1,0:T(8,128)(2,1)} %get-tuple-element.117, bf16[512,2048]{1,0:T(8,128)(2,1)S(1)} %get-tuple-element.116), kind=kOutput, calls=%fused_computation | convolution fusion | flops 2147483648 | bytes 13107200 | tf_op jit(solution)/shard_map/cond/branch_1_fun/dot_general | solution.py:16
  212.6 9.1 %fusion.14 = bf16[512,4096]{1,0:T(8,128)(2,1)} fusion(f32[512,4096]{1,0:T(8,128)} %get-tuple-element.134, bf16[512,4096]{1,0:T(8,128)(2,1)} %param.29, pred[]{:T(512)S(6)} %eq.13, bf16[2048,512]{1,0:T(8,128)(2,1)} %all-gather.2.cloned.1.call-done), kind=kOutput, calls=%fused_computation.26 | convolution fusion | flops 2157969408 | bytes 17301504 | tf_op jit(solution)/shard_map/dot_general | solution.py:39
  221.7 0.0 all-reduce.7.cloned.1.call-update
  221.7 0.0 all-reduce.9.cloned.1.call-start
  223.0 151.3 %all-reduce.7.cloned.1.call-done = bf16[512,4096]{1,0:T(8,128)(2,1)} async-done(((bf16[512,4096]{1,0:T(8,128)(2,1)}), bf16[512,4096]{1,0:T(8,128)(2,1)}) %all-reduce.7.cloned.1.call-update) | async-done | bytes 4194320 | tf_op jit(solution)/shard_map/psum | solution.py:9
  374.3 4.3 conditional.5
  374.3 4.3 broadcast.115
  378.6 0.0 copy-start
  378.6 11.3 %add.59 = f32[512,4096]{1,0:T(8,128)} add(f32[512,4096]{1,0:T(8,128)} %get-tuple-element.134, f32[512,4096]{1,0:T(8,128)} %get-tuple-element.135) | non-fusion elementwise | flops 2097152 | bytes 25165824 | tf_op jit(solution)/shard_map/add | solution.py:46
  389.9 0.0 copy-done
  389.9 8.1 %fusion.16 = bf16[512,4096]{1,0:T(8,128)(2,1)} fusion(f32[512,4096]{1,0:T(8,128)} %add.59, bf16[512,4096]{1,0:T(8,128)(2,1)S(1)} %copy-done, pred[]{:T(512)S(6)} %eq.14, bf16[2048,512]{1,0:T(8,128)(2,1)} %all-gather.2.cloned.1.call-done), kind=kOutput, calls=%fused_computation.28 | convolution fusion | flops 2157969408 | bytes 17301504 | tf_op jit(solution)/shard_map/dot_general | solution.py:39
  398.0 0.0 all-reduce.9.cloned.1.call-update
  398.0 0.0 all-reduce.11.cloned.1.call-start
  399.3 154.3 %all-reduce.9.cloned.1.call-done = bf16[512,4096]{1,0:T(8,128)(2,1)} async-done(((bf16[512,4096]{1,0:T(8,128)(2,1)}), bf16[512,4096]{1,0:T(8,128)(2,1)}) %all-reduce.9.cloned.1.call-update) | async-done | bytes 4194320 | tf_op jit(solution)/shard_map/psum | solution.py:9
  553.7 7.8 %conditional.6 = (f32[512,4096]{1,0:T(8,128)}) conditional(s32[]{:T(128)} %bitcast.8, () %tuple.72, (bf16[512,2048]{1,0:T(8,128)(2,1)S(1)}, bf16[512,4096]{1,0:T(8,128)(2,1)}) %tuple.103), branch_computations={%region_7.8_spmd, %region_8.9_spmd} | conditional | flops 2147483648 | bytes 13107208 | solution.py:14
  553.7 7.8 %fusion.4 = f32[512,4096]{1,0:T(8,128)} fusion(bf16[512,4096]{1,0:T(8,128)(2,1)} %get-tuple-element.121, bf16[512,2048]{1,0:T(8,128)(2,1)S(1)} %get-tuple-element.120), kind=kOutput, calls=%fused_computation.4 | convolution fusion | flops 2147483648 | bytes 13107200 | tf_op jit(solution)/shard_map/cond/branch_1_fun/dot_general | solution.py:16
  561.4 0.0 copy-start.1
  561.4 11.3 %add.60 = f32[512,4096]{1,0:T(8,128)} add(f32[512,4096]{1,0:T(8,128)} %add.59, f32[512,4096]{1,0:T(8,128)} %get-tuple-element.136) | non-fusion elementwise | flops 2097152 | bytes 25165824 | tf_op jit(solution)/shard_map/add | solution.py:46
  572.7 0.0 copy-done.1
  572.7 8.1 %fusion.18 = bf16[512,4096]{1,0:T(8,128)(2,1)} fusion(f32[512,4096]{1,0:T(8,128)} %add.60, bf16[512,4096]{1,0:T(8,128)(2,1)S(1)} %copy-done.1, pred[]{:T(512)S(6)} %eq.15, bf16[2048,512]{1,0:T(8,128)(2,1)} %all-gather.2.cloned.1.call-done), kind=kOutput, calls=%fused_computation.30 | convolution fusion | flops 2157969408 | bytes 17301504 | tf_op jit(solution)/shard_map/dot_general | solution.py:39
  580.9 0.0 all-reduce.11.cloned.1.call-update
  581.5 151.9 %all-reduce.11.cloned.1.call-done = bf16[512,4096]{1,0:T(8,128)(2,1)} async-done(((bf16[512,4096]{1,0:T(8,128)(2,1)}), bf16[512,4096]{1,0:T(8,128)(2,1)}) %all-reduce.11.cloned.1.call-update) | async-done | bytes 4194320 | tf_op jit(solution)/shard_map/psum | solution.py:9
  733.5 7.8 %conditional.7 = (f32[512,4096]{1,0:T(8,128)}) conditional(s32[]{:T(128)} %bitcast.10, () %tuple.74, (bf16[512,2048]{1,0:T(8,128)(2,1)S(1)}, bf16[512,4096]{1,0:T(8,128)(2,1)}) %tuple.104), branch_computations={%region_10.11_spmd, %region_11.12_spmd} | conditional | flops 2147483648 | bytes 13107208 | solution.py:14
  733.5 7.8 %fusion.6 = f32[512,4096]{1,0:T(8,128)} fusion(bf16[512,4096]{1,0:T(8,128)(2,1)} %get-tuple-element.123, bf16[512,2048]{1,0:T(8,128)(2,1)S(1)} %get-tuple-element.122), kind=kOutput, calls=%fused_computation.6 | convolution fusion | flops 2147483648 | bytes 13107200 | tf_op jit(solution)/shard_map/cond/branch_1_fun/dot_general | solution.py:16
  741.3 11.3 %fusion.11 = bf16[512,4096]{1,0:T(8,128)(2,1)} fusion(bf16[512,4096]{1,0:T(8,128)(2,1)} %param.29, f32[512,4096]{1,0:T(8,128)} %add.60, f32[512,4096]{1,0:T(8,128)} %get-tuple-element.137), kind=kLoop, calls=%fused_computation.19 | loop fusion | flops 8388608 | bytes 25165824 | tf_op jit(solution)/shard_map/convert_element_type | solution.py:48
  752.6 1.7 fusion.28
Async XLA Ops:
  7.2 36.8 %all-gather.2.cloned.1.call-start = ((), (), s32[]{:S(2)}) async-start(), calls=%async_computation | async-start | bytes 2621440 | tf_op jit(solution)/shard_map/all_gather | solution.py:28
  7.9 196.9 %all-reduce.5.cloned.1.call-start = ((), (), s32[]{:S(2)}) async-start(), calls=%async_computation.1 | async-start | bytes 8388608 | tf_op jit(solution)/shard_map/psum | solution.py:9
  50.7 0.7 copy-start.3
  50.7 154.1 %copy-start.2 = (bf16[512,2048]{1,0:T(8,128)(2,1)S(1)}, bf16[512,2048]{1,0:T(8,128)(2,1)}, u32[]{:S(2)}) copy-start(bf16[512,2048]{1,0:T(8,128)(2,1)} %param.30) | copy-start | bytes 6291460
  50.7 323.6 %all-reduce.7.cloned.1.call-start = ((), (), s32[]{:S(2)}) async-start(), calls=%async_computation.2 | async-start | bytes 8388608 | tf_op jit(solution)/shard_map/psum | solution.py:9
  221.7 331.9 %all-reduce.9.cloned.1.call-start = ((), (), s32[]{:S(2)}) async-start(), calls=%async_computation.3 | async-start | bytes 8388608 | tf_op jit(solution)/shard_map/psum | solution.py:9
  378.6 11.3 %copy-start = (bf16[512,4096]{1,0:T(8,128)(2,1)S(1)}, bf16[512,4096]{1,0:T(8,128)(2,1)}, u32[]{:S(2)}) copy-start(bf16[512,4096]{1,0:T(8,128)(2,1)} %param.29) | copy-start | bytes 12582916
  398.0 335.4 %all-reduce.11.cloned.1.call-start = ((), (), s32[]{:S(2)}) async-start(), calls=%async_computation.4 | async-start | bytes 8388608 | tf_op jit(solution)/shard_map/psum | solution.py:9
  561.4 11.3 %copy-start.1 = (bf16[512,4096]{1,0:T(8,128)(2,1)S(1)}, bf16[512,4096]{1,0:T(8,128)(2,1)}, u32[]{:S(2)}) copy-start(bf16[512,4096]{1,0:T(8,128)(2,1)} %param.29) | copy-start | bytes 12582916
Sparse Core Ops, SparseCore 0:
  9.7 34.2 all-gather.1
  50.8 153.9 all-reduce.4
  221.9 152.4 all-reduce.6
  398.1 155.4 all-reduce.8
  581.0 152.4 all-reduce.10
where the time goes:
time: 761 us
  waiting for transfers between devices  644 us (85%)
  matrix products  55.5 us (7%)
  other arithmetic  35.6 us (5%)
  between operations  18.9 us (2%)
    psum x4, waiting for transfers between devices, spread(): return lax.psum(block, axis)  609 us
    all_gather x1, waiting for transfers between devices, body(): lax.all_gather(diag_inverse, 'col', axis=0, tiled=True)  33.9 us
    dot_general x4, matrix products, body(): jnp.dot(inverses[k], rounded, preferred_element_type=jnp.float32)  32.1 us
    dot_general x3, matrix products, tile_term(): jnp.dot(tile, panel_solution, preferred_element_type=jnp.float32)  23.4 us
    add x2, other arithmetic, body(): accum = accum.at[0:panel].add(term)  22.6 us
  transfers between devices with their start and end apart: 5, of which 5 were waited for; matrix products, arithmetic and copies ran while one was open for 0% of the time, Pallas kernels for 0%

commit v1 on v0

--- a/solution.py
+++ b/solution.py
@@ -2,6 +2,22 @@
 import jax.numpy as jnp
 from jax import lax
 from jax.sharding import PartitionSpec as P
+
+
+def gather_around(x, axis, dim):
+    ways, here, step = (lax.axis_size(axis), lax.axis_index(axis), x.shape[dim])
+    shape = [n * ways if d == dim else n for d, n in enumerate(x.shape)]
+    full = lax.dynamic_update_slice_in_dim(jnp.zeros(shape, x.dtype), x, here * step, axis=dim)
+    going_up = going_down = x
+    for far in range(1, ways // 2 + 1):
+        going_up = lax.ppermute(going_up, axis, [(d, (d + 1) % ways) for d in range(ways)])
+        full = lax.dynamic_update_slice_in_dim(full, going_up, (here - far) % ways * step, axis=dim)
+        if 2 * far < ways:
+            going_down = lax.ppermute(going_down, axis, [(d, (d - 1) % ways) for d in range(ways)])
+            full = lax.dynamic_update_slice_in_dim(
+                full, going_down, (here + far) % ways * step, axis=dim
+            )
+    return full
 
 
 def spread(block, axis, source):
@@ -25,7 +41,7 @@
     columns = right_side.shape[1]
     ncol = lax.axis_size("col")
     nrow = lax.axis_size("row")
-    inverses = lax.all_gather(diag_inverse, "col", axis=0, tiled=True).reshape(window, panel, panel)
+    inverses = gather_around(diag_inverse, "col", 0).reshape(window, panel, panel)
     col_index = lax.axis_index("col")
     row_index = lax.axis_index("row")
     accum = jnp.zeros((pan_dev * panel, columns), jnp.float32)

time: 761 us -> 754 us (level)
  waiting for transfers between devices: 644 us -> 630 us
    all_gather x1 -> x0, waiting for transfers between devices: 33.9 us -> none  [body(): lax.all_gather(diag_inverse, 'col', axis=0, tiled=True)]
    ppermute x0 -> x3, waiting for transfers between devices: none -> 20.6 us  [the longest x2 20.6 us: gather_around(): lax.ppermute(going_up, axis, [(d, (d + 1) % ways) for d in range(ways)])]
  transfers between devices with their start and end apart: 5 -> 7, of which waited for: 5 -> 6; matrix products, arithmetic and copies ran while one was open for 0% -> 1% of each run, Pallas kernels for 0% -> 0%
where the time goes in v1:
time: 754 us
  waiting for transfers between devices  630 us (84%)
  matrix products  53 us (7%)
  other arithmetic  35.6 us (5%)
  between operations  19 us (3%)
  local copies, waits for them, and re-layouts  10.6 us (1%)
    psum x4, waiting for transfers between devices, spread(): return lax.psum(block, axis)  610 us
    dot_general x4, matrix products, body(): jnp.dot(inverses[k], rounded, preferred_element_type=jnp.float32)  29.2 us
    dot_general x3, matrix products, tile_term(): jnp.dot(tile, panel_solution, preferred_element_type=jnp.float32)  23.9 us
    add x2, other arithmetic, body(): accum = accum.at[0:panel].add(term)  22.6 us
    ppermute x2, waiting for transfers between devices, gather_around(): lax.ppermute(going_up, axis, [(d, (d + 1) % ways) for d in range(ways)])  20.6 us
  transfers between devices with their start and end apart: 7, of which 6 were waited for; matrix products, arithmetic and copies ran while one was open for 1% of the time, Pallas kernels for 0%

profile of v1, /device:TPU:1, one launch (start us, length us, event | category | flops | bytes accessed | tf_op | source)
XLA Modules:
  0.0 753.5 jit_solution(12515864056173875590)
XLA Ops:
  7.2 0.0 all-reduce.5.cloned.1.call-start
  7.2 2.5 collective-permute-start
  9.7 2.2 collective-permute-start.1
  11.9 11.8 %collective-permute-done = bf16[512,512]{1,0:T(8,128)(2,1)S(1)} collective-permute-done((bf16[512,512]{1,0:T(8,128)(2,1)}, bf16[512,512]{1,0:T(8,128)(2,1)S(1)}, u32[]{:S(2)}, u32[]{:S(2)}) %collective-permute-start) | collective-permute-done | bytes 524320 | tf_op jit(solution)/shard_map/ppermute | solution.py:13
  23.7 0.0 collective-permute-start.2
  23.7 1.5 fusion.27
  25.8 0.0 copy-start
  25.9 0.1 broadcast_in_dim.3
  26.0 1.2 constant_dynamic-update-slice_fusion.3
  27.3 0.0 collective-permute-done.1
  27.3 1.1 constant_dynamic-update-slice_fusion.1
  28.4 8.8 %collective-permute-done.2 = bf16[512,512]{1,0:T(8,128)(2,1)} collective-permute-done((bf16[512,512]{1,0:T(8,128)(2,1)S(1)}, bf16[512,512]{1,0:T(8,128)(2,1)}, u32[]{:S(2)}, u32[]{:S(2)}) %collective-permute-start.2) | collective-permute-done | bytes 524320 | tf_op jit(solution)/shard_map/ppermute | solution.py:13
  37.2 1.1 constant_dynamic-update-slice_fusion
  38.3 0.0 copy-done
  38.3 4.4 fusion.12
  42.7 0.0 copy-start.3
  42.7 0.0 all-reduce.5.cloned.1.call-update
  42.7 0.0 all-reduce.7.cloned.1.call-start
  42.8 0.6 copy-done.3
  43.3 0.7 fusion.26
  45.3 152.0 %all-reduce.5.cloned.1.call-done = bf16[512,4096]{1,0:T(8,128)(2,1)} async-done(((bf16[512,4096]{1,0:T(8,128)(2,1)}), bf16[512,4096]{1,0:T(8,128)(2,1)}) %all-reduce.5.cloned.1.call-update) | async-done | bytes 4194320 | tf_op jit(solution)/shard_map/psum | solution.py:25
  197.4 8.0 %conditional.4 = (f32[512,4096]{1,0:T(8,128)}) conditional(s32[]{:T(128)} %bitcast.2, () %tuple.68, (bf16[512,2048]{1,0:T(8,128)(2,1)}, bf16[512,4096]{1,0:T(8,128)(2,1)}) %tuple.69), branch_computations={%region_1.2_spmd, %region_2.3_spmd} | conditional | flops 2147483648 | bytes 13107208 | solution.py:30
  197.4 8.0 %fusion = f32[512,4096]{1,0:T(8,128)} fusion(bf16[512,4096]{1,0:T(8,128)(2,1)} %get-tuple-element.117, bf16[512,2048]{1,0:T(8,128)(2,1)} %get-tuple-element.116), kind=kOutput, calls=%fused_computation | convolution fusion | flops 2147483648 | bytes 13107200 | tf_op jit(solution)/shard_map/cond/branch_1_fun/dot_general | solution.py:32
  205.3 9.0 %fusion.13 = bf16[512,4096]{1,0:T(8,128)(2,1)} fusion(f32[512,4096]{1,0:T(8,128)} %get-tuple-element.134, bf16[512,4096]{1,0:T(8,128)(2,1)} %param.29, pred[]{:T(512)S(6)} %eq.17, bf16[2048,512]{1,0:T(8,128)(2,1)S(1)} %constant_dynamic-update-slice_fusion), kind=kOutput, calls=%fused_computation.25 | convolution fusion | flops 2157969408 | bytes 17301504 | tf_op jit(solution)/shard_map/dot_general | solution.py:55
  214.3 0.0 all-reduce.7.cloned.1.call-update
  214.3 0.0 all-reduce.9.cloned.1.call-start
  215.6 151.3 %all-reduce.7.cloned.1.call-done = bf16[512,4096]{1,0:T(8,128)(2,1)} async-done(((bf16[512,4096]{1,0:T(8,128)(2,1)}), bf16[512,4096]{1,0:T(8,128)(2,1)}) %all-reduce.7.cloned.1.call-update) | async-done | bytes 4194320 | tf_op jit(solution)/shard_map/psum | solution.py:25
  366.9 4.3 conditional.5
  366.9 4.3 broadcast.107
  371.1 0.0 copy-start.1
  371.1 11.3 %add.94 = f32[512,4096]{1,0:T(8,128)} add(f32[512,4096]{1,0:T(8,128)} %get-tuple-element.134, f32[512,4096]{1,0:T(8,128)} %get-tuple-element.135) | non-fusion elementwise | flops 2097152 | bytes 25165824 | tf_op jit(solution)/shard_map/add | solution.py:62
  382.4 0.0 copy-done.1
  382.4 7.9 %fusion.14 = bf16[512,4096]{1,0:T(8,128)(2,1)} fusion(f32[512,4096]{1,0:T(8,128)} %add.94, bf16[512,4096]{1,0:T(8,128)(2,1)S(1)} %copy-done.1, pred[]{:T(512)S(6)} %eq.18, bf16[2048,512]{1,0:T(8,128)(2,1)S(1)} %constant_dynamic-update-slice_fusion), kind=kOutput, calls=%fused_computation.26 | convolution fusion | flops 2157969408 | bytes 17301504 | tf_op jit(solution)/shard_map/dot_general | solution.py:55
  390.4 0.0 all-reduce.9.cloned.1.call-update
  390.4 0.0 all-reduce.11.cloned.1.call-start
  391.7 154.5 %all-reduce.9.cloned.1.call-done = bf16[512,4096]{1,0:T(8,128)(2,1)} async-done(((bf16[512,4096]{1,0:T(8,128)(2,1)}), bf16[512,4096]{1,0:T(8,128)(2,1)}) %all-reduce.9.cloned.1.call-update) | async-done | bytes 4194320 | tf_op jit(solution)/shard_map/psum | solution.py:25
  546.2 8.0 %conditional.6 = (f32[512,4096]{1,0:T(8,128)}) conditional(s32[]{:T(128)} %bitcast.6, () %tuple.72, (bf16[512,2048]{1,0:T(8,128)(2,1)}, bf16[512,4096]{1,0:T(8,128)(2,1)}) %tuple.73), branch_computations={%region_7.8_spmd, %region_8.9_spmd} | conditional | flops 2147483648 | bytes 13107208 | solution.py:30
  546.2 8.0 %fusion.4 = f32[512,4096]{1,0:T(8,128)} fusion(bf16[512,4096]{1,0:T(8,128)(2,1)} %get-tuple-element.121, bf16[512,2048]{1,0:T(8,128)(2,1)} %get-tuple-element.120), kind=kOutput, calls=%fused_computation.4 | convolution fusion | flops 2147483648 | bytes 13107200 | tf_op jit(solution)/shard_map/cond/branch_1_fun/dot_general | solution.py:32
  554.2 0.0 copy-start.2
  554.2 11.3 %add.95 = f32[512,4096]{1,0:T(8,128)} add(f32[512,4096]{1,0:T(8,128)} %add.94, f32[512,4096]{1,0:T(8,128)} %get-tuple-element.136) | non-fusion elementwise | flops 2097152 | bytes 25165824 | tf_op jit(solution)/shard_map/add | solution.py:62
  565.5 0.0 copy-done.2
  565.5 7.9 %fusion.15 = bf16[512,4096]{1,0:T(8,128)(2,1)} fusion(f32[512,4096]{1,0:T(8,128)} %add.95, bf16[512,4096]{1,0:T(8,128)(2,1)S(1)} %copy-done.2, pred[]{:T(512)S(6)} %eq.19, bf16[2048,512]{1,0:T(8,128)(2,1)S(1)} %constant_dynamic-update-slice_fusion), kind=kOutput, calls=%fused_computation.27 | convolution fusion | flops 2157969408 | bytes 17301504 | tf_op jit(solution)/shard_map/dot_general | solution.py:55
  573.4 0.0 all-reduce.11.cloned.1.call-update
  574.1 151.9 %all-reduce.11.cloned.1.call-done = bf16[512,4096]{1,0:T(8,128)(2,1)} async-done(((bf16[512,4096]{1,0:T(8,128)(2,1)}), bf16[512,4096]{1,0:T(8,128)(2,1)}) %all-reduce.11.cloned.1.call-update) | async-done | bytes 4194320 | tf_op jit(solution)/shard_map/psum | solution.py:25
  726.0 8.0 %conditional.7 = (f32[512,4096]{1,0:T(8,128)}) conditional(s32[]{:T(128)} %bitcast.7, () %tuple.74, (bf16[512,2048]{1,0:T(8,128)(2,1)}, bf16[512,4096]{1,0:T(8,128)(2,1)}) %tuple.75), branch_computations={%region_10.11_spmd, %region_11.12_spmd} | conditional | flops 2147483648 | bytes 13107208 | solution.py:30
  726.0 8.0 %fusion.6 = f32[512,4096]{1,0:T(8,128)} fusion(bf16[512,4096]{1,0:T(8,128)(2,1)} %get-tuple-element.123, bf16[512,2048]{1,0:T(8,128)(2,1)} %get-tuple-element.122), kind=kOutput, calls=%fused_computation.6 | convolution fusion | flops 2147483648 | bytes 13107200 | tf_op jit(solution)/shard_map/cond/branch_1_fun/dot_general | solution.py:32
  734.0 11.3 %fusion.11 = bf16[512,4096]{1,0:T(8,128)(2,1)} fusion(bf16[512,4096]{1,0:T(8,128)(2,1)} %param.29, f32[512,4096]{1,0:T(8,128)} %add.95, f32[512,4096]{1,0:T(8,128)} %get-tuple-element.137), kind=kLoop, calls=%fused_computation.19 | loop fusion | flops 8388608 | bytes 25165824 | tf_op jit(solution)/shard_map/convert_element_type | solution.py:64
  745.3 1.7 fusion.25
  (1 shorter events, 0.0 us)
Async XLA Ops:
  7.2 190.2 %all-reduce.5.cloned.1.call-start = ((), (), s32[]{:S(2)}) async-start(), calls=%async_computation | async-start | bytes 8388608 | tf_op jit(solution)/shard_map/psum | solution.py:25
  7.2 16.5 %collective-permute-start = (bf16[512,512]{1,0:T(8,128)(2,1)}, bf16[512,512]{1,0:T(8,128)(2,1)S(1)}, u32[]{:S(2)}, u32[]{:S(2)}) collective-permute-start(bf16[512,512]{1,0:T(8,128)(2,1)} %param.31), channel_id=1, source_target_pairs={{0,1},{1,2},{2,3},{3,0},{4,5},{5,6},{6,7},{7,4},{8,9},{9,10},{10,1... | collective-permute-start | bytes 1572872 | tf_op jit(solution)/shard_map/ppermute | solution.py:13
  9.7 17.5 %collective-permute-start.1 = (bf16[512,512]{1,0:T(8,128)(2,1)}, bf16[512,512]{1,0:T(8,128)(2,1)}, u32[]{:S(2)}, u32[]{:S(2)}) collective-permute-start(bf16[512,512]{1,0:T(8,128)(2,1)} %param.31), channel_id=1, source_target_pairs={{0,3},{1,0},{2,1},{3,2},{4,7},{5,4},{6,5},{7,6},{8,11},{9,8},{10,9... | collective-permute-start | bytes 1572872 | tf_op jit(solution)/shard_map/ppermute | solution.py:16
  23.7 13.5 %collective-permute-start.2 = (bf16[512,512]{1,0:T(8,128)(2,1)S(1)}, bf16[512,512]{1,0:T(8,128)(2,1)}, u32[]{:S(2)}, u32[]{:S(2)}) collective-permute-start(bf16[512,512]{1,0:T(8,128)(2,1)S(1)} %collective-permute-done), channel_id=1, source_target_pairs={{0,1},{1,2},{2,3},{3,0},{4,5},{5,6},{6,7},{7,4},{8,9},{9,10},{10,1... | collective-permute-start | bytes 1572872 | tf_op jit(solution)/shard_map/ppermute | solution.py:13
  25.8 12.5 %copy-start = (bf16[512,4096]{1,0:T(8,128)(2,1)S(1)}, bf16[512,4096]{1,0:T(8,128)(2,1)}, u32[]{:S(2)}) copy-start(bf16[512,4096]{1,0:T(8,128)(2,1)} %param.29) | copy-start | bytes 12582916
  42.7 0.7 copy-start.3
  42.7 324.2 %all-reduce.7.cloned.1.call-start = ((), (), s32[]{:S(2)}) async-start(), calls=%async_computation.1 | async-start | bytes 8388608 | tf_op jit(solution)/shard_map/psum | solution.py:25
  214.3 331.9 %all-reduce.9.cloned.1.call-start = ((), (), s32[]{:S(2)}) async-start(), calls=%async_computation.2 | async-start | bytes 8388608 | tf_op jit(solution)/shard_map/psum | solution.py:25
  371.1 11.3 %copy-start.1 = (bf16[512,4096]{1,0:T(8,128)(2,1)S(1)}, bf16[512,4096]{1,0:T(8,128)(2,1)}, u32[]{:S(2)}) copy-start(bf16[512,4096]{1,0:T(8,128)(2,1)} %param.29) | copy-start | bytes 12582916
  390.4 335.6 %all-reduce.11.cloned.1.call-start = ((), (), s32[]{:S(2)}) async-start(), calls=%async_computation.3 | async-start | bytes 8388608 | tf_op jit(solution)/shard_map/psum | solution.py:25
  554.2 11.3 %copy-start.2 = (bf16[512,4096]{1,0:T(8,128)(2,1)S(1)}, bf16[512,4096]{1,0:T(8,128)(2,1)}, u32[]{:S(2)}) copy-start(bf16[512,4096]{1,0:T(8,128)(2,1)} %param.29) | copy-start | bytes 12582916
Sparse Core Ops, SparseCore 0:
  42.8 154.4 all-reduce.4
  214.4 152.4 all-reduce.6
  390.5 155.6 all-reduce.8
  573.5 152.4 all-reduce.10
